TPU v7x, 32 devices: a whole 2x2x4 slice. The times are simulated.
32 devices in a mesh: row: 8 (over y, x, core), col: 4 (over z).
Axes of the slice: x: 2, y: 2, z: 4, core: 2. Of those that a mesh axis runs over, the one named last changes fastest.
Arguments:
- tokens: bfloat16 [128, 96, 768], P('row', 'col'), as said below
- dw_kernel: float32 [7, 7, 768], replicated, may hold values from -0.875 to 0.875
- norm_gain: float32 [768], replicated, may hold values from 0.5 to 1.5
- norm_shift: float32 [768], replicated, may hold values from -3 to 3
- w_in: bfloat16 [768, 3072], P(None, 'col'), may hold values from -0.21875 to 0.21875
- w_out: bfloat16 [3072, 768], P('col'), may hold values from -0.109375 to 0.109375
- w_kv: bfloat16 [768, 1536], P(None, 'col'), as said below
- queries: bfloat16 [512, 768], replicated, may hold values from -300 to 300, as said below
- latent_gain: float32 [768], replicated, may hold values from 0.5 to 1.5
- w_o: bfloat16 [768, 768], P(None, 'col'), may hold values from -0.21875 to 0.21875
Outputs:
- token_map: bfloat16 [128, 96, 768], P('row', 'col')
- latents: bfloat16 [512, 768], replicated
Inputs may be any that keep to these rules, and one draw needn't show every extreme that they name: Latent queries; a few rows may be far larger than the others. `tokens`: patch token features, roughly unit normal, between -24 and 24; a few cells hold 24 in two channels. `w_kv`: key and value projection weights.
All inputs are finite; a program needn't handle non-finite values.
Results may differ from a plain program's by a relative error of at most 0.011.
Values may be sent and summed in bfloat16 or wider, within the bound.
A program may use at most 64 MiB of HBM per device.

v0:
```python
import math
import jax
import jax.numpy as jnp
from jax import lax
from jax.sharding import PartitionSpec as P

HEADS = 12
HEAD = 64


def with_halo(cells, sides, width):
    for axis, dim in sides:
        count = lax.axis_size(axis)
        ends = count - 1
        head = lax.slice_in_dim(cells, 0, width, axis=dim)
        tail = lax.slice_in_dim(cells, cells.shape[dim] - width, cells.shape[dim], axis=dim)
        cells = jnp.concatenate(
            [
                lax.ppermute(tail, axis, [(i, (i + 1) % count) for i in range(ends)]),
                cells,
                lax.ppermute(head, axis, [((i + 1) % count, i) for i in range(ends)]),
            ],
            axis=dim,
        )
    return cells


def conv_taps(padded, height, width, dw_kernel):
    mixed = jnp.zeros((height, width, padded.shape[2]), jnp.float32)
    for row_tap in range(7):
        for col_tap in range(7):
            mixed = (
                mixed
                + padded[row_tap : row_tap + height, col_tap : col_tap + width]
                * dw_kernel[row_tap, col_tap]
            )
    return mixed


def layer_norm(mixed, norm_gain, norm_shift):
    center = mixed - jnp.mean(mixed, axis=-1, keepdims=True)
    spread = jnp.mean(center * center, axis=-1, keepdims=True)
    return (center * lax.rsqrt(spread + 1e-06) * norm_gain + norm_shift).astype(jnp.bfloat16)


def finish_latents(numer, denom, latent_gain, w_full):
    attended = (numer / denom[..., None]).reshape(numer.shape[0], -1)
    squares = jnp.mean(attended * attended, axis=-1, keepdims=True)
    scaled = (attended * lax.rsqrt(squares + 1e-06) * latent_gain).astype(jnp.bfloat16)
    return jnp.dot(scaled, w_full, preferred_element_type=jnp.float32).astype(jnp.bfloat16)


def body(tokens, dw_kernel, norm_gain, norm_shift, w_in, w_out, w_kv, queries, latent_gain, w_o):
    height, width, width_d = tokens.shape
    latent_count = queries.shape[0]
    padded = with_halo(tokens, (("row", 0), ("col", 1)), 3)
    mixed = conv_taps(padded.astype(jnp.float32), height, width, dw_kernel)
    normed = layer_norm(mixed, norm_gain, norm_shift).reshape(height * width, width_d)
    residual = tokens.reshape(height * width, width_d).astype(jnp.float32)
    hidden = jax.nn.gelu(
        jnp.dot(
            normed,
            lax.all_gather(w_in, "col", axis=1, tiled=True),
            preferred_element_type=jnp.float32,
        )
    ).astype(jnp.bfloat16)
    update = jnp.dot(
        hidden, lax.all_gather(w_out, "col", axis=0, tiled=True), preferred_element_type=jnp.float32
    )
    token_rows = (residual + update).astype(jnp.bfloat16)
    token_map = token_rows.reshape(height, width, width_d)
    keys_vals = jnp.dot(
        token_rows,
        lax.all_gather(w_kv, "col", axis=1, tiled=True),
        preferred_element_type=jnp.float32,
    ).astype(jnp.bfloat16)
    w_full = lax.all_gather(w_o, "col", axis=1, tiled=True)
    key_heads = keys_vals[:, :width_d].reshape(-1, HEADS, HEAD)
    val_heads = keys_vals[:, width_d:].reshape(-1, HEADS, HEAD)
    query_heads = queries.reshape(latent_count, HEADS, HEAD)
    score_scale = 1.0 / math.sqrt(HEAD)
    group_size = math.gcd(HEADS, 4)
    max_parts, den_parts, num_parts = ([], [], [])
    for first_head in range(0, HEADS, group_size):
        scores = (
            jnp.einsum(
                "lhd,thd->lht",
                query_heads[:, first_head : first_head + group_size],
                key_heads[:, first_head : first_head + group_size],
                preferred_element_type=jnp.float32,
            )
            * score_scale
        )
        local_max = jnp.max(scores, axis=-1)
        weights = jnp.exp(scores - local_max[..., None])
        den_parts.append(jnp.sum(weights, axis=-1))
        max_parts.append(local_max)
        num_parts.append(
            jnp.einsum(
                "lht,thd->lhd",
                weights.astype(jnp.bfloat16),
                val_heads[:, first_head : first_head + group_size],
                preferred_element_type=jnp.float32,
            )
        )
    maxima = jnp.concatenate(max_parts, axis=1)
    denom = jnp.concatenate(den_parts, axis=1)
    numer = jnp.concatenate(num_parts, axis=1)
    peak = lax.pmax(maxima, ("row", "col"))
    factor = jnp.exp(maxima - peak)
    den_terms = denom * factor
    num_terms = (numer * factor[..., None]).reshape(latent_count, width_d)
    den_part, num_part = (
        lax.psum_scatter(den_terms, "col", scatter_dimension=0, tiled=True),
        lax.psum_scatter(num_terms, "col", scatter_dimension=0, tiled=True),
    )
    den_share, num_share = lax.psum((den_part, num_part), "row")
    own_rows = finish_latents(
        num_share.reshape(num_share.shape[0], HEADS, HEAD), den_share, latent_gain, w_full
    )
    latents = lax.all_gather(own_rows, "col", axis=0, tiled=True)
    return (token_map, latents)


def solution(mesh):
    in_specs = (
        P("row", "col", None),
        P(),
        P(),
        P(),
        P(None, "col"),
        P("col", None),
        P(None, "col"),
        P(),
        P(),
        P(None, "col"),
    )
    out_specs = (P("row", "col", None), P())
    return jax.shard_map(body, mesh=mesh, in_specs=in_specs, out_specs=out_specs, check_vma=False)
```

profile of v0, /device:TPU:0, one launch (start us, length us, event | category | flops | bytes accessed | tf_op | source)
XLA Modules:
  0.0 479.7 jit_solution(5248755326156885472)
XLA Ops:
  8.8 2.4 collective-permute-start
  11.2 1.3 collective-permute-start.1
  12.7 1.2 copy.24
  14.1 2.3 collective-permute-done.1
  16.6 3.5 collective-permute-start.2
  20.1 1.3 collective-permute-start.3
  21.5 4.3 collective-permute-done.2
  25.8 7.4 %collective-permute-done.3 = bf16[22,3,768]{2,1,0:T(4,128)(2,1)S(1)} collective-permute-done((bf16[22,3,768]{2,1,0:T(4,128)(2,1)S(1)}, bf16[22,3,768]{2,1,0:T(4,128)(2,1)S(1)}, u32[]{:S(2)}, u32[]{:S(2)}) %collective-permute-start.3) | collective-permute-done | bytes 101408 | tf_op jit(solution)/shard_map/ppermute | solution.py:21
  33.6 12.3 %fusion.109 = (f32[16,24]{1,0:T(8,128)S(1)}, f32[16,24,768]{2,1,0:T(8,128)S(1)}) fusion(f32[768]{0:T(1024)S(1)} %get-tuple-element.49, f32[22,30,768]{2,1,0:T(8,128)S(1)} %maximum_convert_fusion, f32[768]{0:T(1024)S(1)} %get-tuple-element.50, f32[768]{0:T(1024)S(1)} %get-tuple-element.3, f32[768]{0:T(1024)S(1)} %get-tuple-element.4, ...), kind=kLoop, calls=%fused_computation.218 | loop fusion | flops 28900992 | bytes 59134464 | tf_op jit(solution)/shard_map/reduce_sum | solution.py:41
  46.8 57.7 %all-gather.5.cloned.1.call-done = bf16[768,3072]{1,0:T(8,128)(2,1)} async-done(((bf16[768,768]{1,0:T(8,128)(2,1)}), bf16[768,3072]{1,0:T(8,128)(2,1)}) %all-gather.5.cloned.1.call-update) | async-done | bytes 4718608 | tf_op jit(solution)/shard_map/all_gather | solution.py:63
  104.6 89.4 %all-gather.7.cloned.1.call-done = bf16[3072,768]{1,0:T(8,128)(2,1)} async-done(((bf16[768,768]{1,0:T(8,128)(2,1)}), bf16[3072,768]{1,0:T(8,128)(2,1)}) %all-gather.7.cloned.1.call-update) | async-done | bytes 4718608 | tf_op jit(solution)/shard_map/all_gather | solution.py:68
  193.9 7.9 %fusion.34 = bf16[384,768]{1,0:T(8,128)(2,1)S(1)} fusion(bf16[3072,768]{1,0:T(8,128)(2,1)} %all-gather.7.cloned.1.call-done, bf16[384,768]{1,0:T(8,128)(2,1)S(1)} %bitcast.66, bf16[384,768]{1,0:T(8,128)(2,1)S(1)} %bitcast.70, bf16[768,3072]{1,0:T(8,128)(2,1)} %all-gather.5.cloned.1.call-done), kind=kOutput, calls=%fused_computation.37 | convolution fusion | flops 3635380224 | bytes 11206656 | tf_op jit(solution)/shard_map/dot_general | solution.py:67
  201.9 42.4 %all-gather.9.cloned.1.call-done = bf16[768,1536]{1,0:T(8,128)(2,1)} async-done(((bf16[768,384]{1,0:T(8,128)(2,1)}), bf16[768,1536]{1,0:T(8,128)(2,1)}) %all-gather.9.cloned.1.call-update) | async-done | bytes 2359312 | tf_op jit(solution)/shard_map/all_gather | solution.py:74
  244.2 2.7 convolution_convert_fusion
  248.9 1.8 bitcast_reduce_fusion
  250.8 2.3 bitcast_reduce_fusion.1
  253.0 2.3 bitcast_reduce_fusion.2
  255.4 2.1 copy.22
  257.5 3.6 fusion.37
  261.1 3.0 fusion.11
  264.1 1.5 fusion.40
  266.2 1.5 fusion.43
  267.6 39.0 %pmax.7 = f32[512,12]{0,1:T(8,128)S(1)} all-reduce(f32[512,12]{0,1:T(8,128)S(1)} %pad_maximum_fusion), channel_id=1, replica_groups=mesh['row'=8,'col'=4] {'row','col'}, use_global_device_ids=true, to_apply=%region_5.0 | all-reduce | flops 6144 | bytes 49152 | tf_op jit(solution)/shard_map/pmax | solution.py:109
  307.3 2.7 maximum_multiply_fusion
  310.6 34.6 %reduce-scatter.3.cloned.1.call-done = f32[128,768]{0,1:T(8,128)} async-done(((f32[512,768]{0,1:T(8,128)}), f32[128,768]{0,1:T(8,128)}) %reduce-scatter.3.cloned.1.call-update) | async-done | bytes 393232 | tf_op jit(solution)/shard_map/reduce_scatter | solution.py:115
  346.0 19.4 %reduce-scatter.5.cloned.1.call-done = f32[128,12]{0,1:T(8,128)} async-done(((f32[512,12]{0,1:T(8,128)}), f32[128,12]{0,1:T(8,128)}) %reduce-scatter.5.cloned.1.call-update) | async-done | bytes 6160 | tf_op jit(solution)/shard_map/reduce_scatter | solution.py:114
  365.4 12.2 %psum.15 = f32[128,12]{0,1:T(8,128)S(1)} all-reduce(f32[128,12]{0,1:T(8,128)} %reduce-scatter.5.cloned.1.call-done), channel_id=1, replica_groups=mesh['row'=8,'col'=4] {'row'}, use_global_device_ids=true, to_apply=%region_12.0 | all-reduce | flops 1536 | bytes 12288 | tf_op jit(solution)/shard_map/psum | solution.py:117
  377.7 43.2 %all-reduce.2.cloned.1.call-done = f32[128,768]{0,1:T(8,128)} async-done(((f32[128,768]{0,1:T(8,128)}), f32[128,768]{0,1:T(8,128)}) %all-reduce.2.cloned.1.call-update) | async-done | bytes 393232 | tf_op jit(solution)/shard_map/psum | solution.py:117
  420.9 1.1 multiply_reduce_fusion.1
  422.0 30.1 %all-gather.11.cloned.1.call-done = bf16[768,768]{0,1:T(8,128)(2,1)} async-done(((bf16[768,192]{0,1:T(8,128)(2,1)}), bf16[768,768]{0,1:T(8,128)(2,1)}) %all-gather.11.cloned.1.call-update) | async-done | bytes 1179664 | tf_op jit(solution)/shard_map/all_gather | solution.py:77
  452.1 1.9 convolution_convert_fusion.1
  454.0 17.9 %all_gather.19 = bf16[512,768]{1,0:T(8,128)(2,1)S(1)} all-gather(bf16[128,768]{1,0:T(8,128)(2,1)S(1)} %convolution_convert_fusion.1), channel_id=1, replica_groups=mesh['row'=8,'col'=4] {'col'}, dimensions={0}, use_global_device_ids=true | all-gather | bytes 983040 | tf_op jit(solution)/shard_map/all_gather | solution.py:121
  (57 shorter events, 8.9 us)
Async XLA Ops:
  7.2 1.6 copy-start.1
  7.2 97.4 %all-gather.5.cloned.1.call-start = ((), (), s32[]{:S(2)}) async-start(), calls=%async_computation.2 | async-start | bytes 5898240 | tf_op jit(solution)/shard_map/all_gather | solution.py:63
  7.9 4.6 copy-start.6
  7.9 4.8 %copy-start.2 = (bf16[512,768]{1,0:T(8,128)(2,1)S(1)}, bf16[512,768]{1,0:T(8,128)(2,1)}, u32[]{:S(2)}) copy-start(bf16[512,768]{1,0:T(8,128)(2,1)} %param.17) | copy-start | bytes 2359300
  7.9 186.0 %all-gather.7.cloned.1.call-start = ((), (), s32[]{:S(2)}) async-start(), calls=%async_computation.3 | async-start | bytes 5898240 | tf_op jit(solution)/shard_map/all_gather | solution.py:68
  8.7 235.6 %all-gather.9.cloned.1.call-start = ((), (), s32[]{:S(2)}) async-start(), calls=%async_computation.4 | async-start | bytes 2949120 | tf_op jit(solution)/shard_map/all_gather | solution.py:74
  8.8 5.3 %collective-permute-start = (bf16[3,24,768]{2,1,0:T(8,128)(2,1)S(1)}, bf16[3,24,768]{2,1,0:T(8,128)(2,1)S(1)}, u32[]{:S(2)}, u32[]{:S(2)}) collective-permute-start(bf16[3,24,768]{2,1,0:T(8,128)(2,1)S(1)} %get-tuple-element.62), channel_id=1, source_target_pairs={{0,4},{4,8},{8,12},{12,16},{16,20},{20,24},{24,28},{1,5},{5,9},{9,... | collective-permute-start | bytes 331784 | tf_op jit(solution)/shard_map/ppermute | solution.py:19
  11.2 5.3 %collective-permute-start.1 = (bf16[3,24,768]{2,1,0:T(8,128)(2,1)S(1)}, bf16[3,24,768]{2,1,0:T(8,128)(2,1)S(1)}, u32[]{:S(2)}, u32[]{:S(2)}) collective-permute-start(bf16[3,24,768]{2,1,0:T(8,128)(2,1)S(1)} %get-tuple-element.61), channel_id=1, source_target_pairs={{4,0},{8,4},{12,8},{16,12},{20,16},{24,20},{28,24},{5,1},{9,5},{13... | collective-permute-start | bytes 331784 | tf_op jit(solution)/shard_map/ppermute | solution.py:21
  12.5 332.7 %reduce-scatter.3.cloned.1.call-start = ((), (), s32[]{:S(2)}) async-start(), calls=%async_computation.5 | async-start | bytes 1966080 | tf_op jit(solution)/shard_map/reduce_scatter | solution.py:115
  16.6 9.2 %collective-permute-start.2 = (bf16[22,3,768]{2,1,0:T(4,128)(2,1)S(1)}, bf16[22,3,768]{2,1,0:T(4,128)(2,1)S(1)}, u32[]{:S(2)}, u32[]{:S(2)}) collective-permute-start(bf16[22,3,768]{2,1,0:T(4,128)(2,1)S(1)} %get-tuple-element.59), channel_id=1, source_target_pairs={{0,1},{1,2},{2,3},{4,5},{5,6},{6,7},{8,9},{9,10},{10,11},{12,13},{... | collective-permute-start | bytes 304136 | tf_op jit(solution)/shard_map/ppermute | solution.py:19
  20.1 13.1 %collective-permute-start.3 = (bf16[22,3,768]{2,1,0:T(4,128)(2,1)S(1)}, bf16[22,3,768]{2,1,0:T(4,128)(2,1)S(1)}, u32[]{:S(2)}, u32[]{:S(2)}) collective-permute-start(bf16[22,3,768]{2,1,0:T(4,128)(2,1)S(1)} %get-tuple-element.60), channel_id=1, source_target_pairs={{1,0},{2,1},{3,2},{5,4},{6,5},{7,6},{9,8},{10,9},{11,10},{13,12},{... | collective-permute-start | bytes 304136 | tf_op jit(solution)/shard_map/ppermute | solution.py:21
  45.9 0.7 copy-start.7
  45.9 0.7 copy-start.8
  201.9 45.1 %copy-start.10 = (bf16[384,768]{1,0:T(8,128)(2,1)}, bf16[384,768]{1,0:T(8,128)(2,1)S(1)}, u32[]{:S(2)}) copy-start(bf16[384,768]{1,0:T(8,128)(2,1)S(1)} %fusion.34) | copy-start | bytes 1769476
  248.9 1.8 copy-start.3
  248.9 1.8 copy-start.5
  257.5 3.6 copy-start
  261.1 3.0 copy-start.4
  310.0 142.2 %copy-start.9 = (f32[768]{0:T(1024)S(1)}, f32[768]{0:T(1024)}, u32[]{:S(2)}) copy-start(f32[768]{0:T(1024)} %param.18) | copy-start | bytes 9220
  310.0 55.4 %reduce-scatter.5.cloned.1.call-start = ((), (), s32[]{:S(2)}) async-start(), calls=%async_computation.7 | async-start | bytes 40960 | tf_op jit(solution)/shard_map/reduce_scatter | solution.py:114
  310.6 110.3 %all-reduce.2.cloned.1.call-start = ((), (), s32[]{:S(2)}) async-start(), calls=%async_computation.6 | async-start | bytes 786432 | tf_op jit(solution)/shard_map/psum | solution.py:117
  345.2 106.9 %all-gather.11.cloned.1.call-start = ((), (), s32[]{:S(2)}) async-start(), calls=%async_computation.8 | async-start | bytes 1474560 | tf_op jit(solution)/shard_map/all_gather | solution.py:77
Sparse Core Ops, SparseCore 0:
  9.6 94.9 all-gather.4
  106.1 87.7 all-gather.6
  195.6 48.6 all-gather.8
  310.1 35.0 reduce-scatter.2
  347.3 18.0 reduce-scatter.4
  368.4 52.5 all-reduce.1
  422.5 29.6 all-gather.10
where the time goes:
time: 480 us
  waiting for transfers between devices  334 us (70%)
  blocking collectives  69.1 us (14%)
  matrix products  25.5 us (5%)
  other arithmetic  21.2 us (4%)
  between operations  14.4 us (3%)
  starting transfers between devices  8.75 us (2%)
  local copies, waits for them, and re-layouts  7.14 us (1%)
    all_gather x1, waiting for transfers between devices, body(): lax.all_gather(w_out, 'col', axis=0, tiled=True)  89.4 us
    all_gather x1, waiting for transfers between devices, body(): lax.all_gather(w_in, 'col', axis=1, tiled=True)  57.7 us
    psum x1, waiting for transfers between devices, body(): den_share, num_share = lax.psum((den_part, num_part), 'row')  43.2 us
    all_gather x1, waiting for transfers between devices, body(): lax.all_gather(w_kv, 'col', axis=1, tiled=True)  42.4 us
    pmax x1, blocking collectives, body(): peak = lax.pmax(maxima, ('row', 'col'))  39 us
    reduce_scatter x1, waiting for transfers between devices, body(): lax.psum_scatter(num_terms, 'col', scatter_dimension=0, tiled=True)  34.6 us
    all_gather x1, waiting for transfers between devices, body(): w_full = lax.all_gather(w_o, 'col', axis=1, tiled=True)  30.1 us
    reduce_scatter x1, waiting for transfers between devices, body(): lax.psum_scatter(den_terms, 'col', scatter_dimension=0, tiled=True)  19.4 us
  transfers between devices with their start and end apart: 11, of which 10 were waited for; matrix products, arithmetic and copies ran while one was open for 5% of the time, Pallas kernels for 0%

commit v1 on v0

--- a/solution.py
+++ b/solution.py
@@ -6,6 +6,12 @@
 
 HEADS = 12
 HEAD = 64
+
+
+def pack_trails(slab_in, axis_k):
+    o_now = list(slab_in.shape[1:])
+    o_now[axis_k] *= slab_in.shape[0]
+    return jnp.moveaxis(slab_in, 0, axis_k).reshape(o_now)
 
 
 def with_halo(cells, sides, width):
@@ -51,6 +57,17 @@
 
 
 def body(tokens, dw_kernel, norm_gain, norm_shift, w_in, w_out, w_kv, queries, latent_gain, w_o):
+
+    def fix_area(arr_in, comm_axis, which_dim=1):
+        ndev = lax.axis_size(comm_axis)
+        frames = list(map(lambda it: (it, (it + 1) % ndev), range(ndev)))
+        series = [arr_in]
+        while len(series) < ndev:
+            series.append(lax.ppermute(series[-1], comm_axis, frames))
+        low = lax.axis_index(comm_axis)
+        series = jnp.stack(series, 0)[(low - jnp.arange(ndev)) % ndev]
+        return pack_trails(series, which_dim)
+
     height, width, width_d = tokens.shape
     latent_count = queries.shape[0]
     padded = with_halo(tokens, (("row", 0), ("col", 1)), 3)
@@ -74,7 +91,7 @@
         lax.all_gather(w_kv, "col", axis=1, tiled=True),
         preferred_element_type=jnp.float32,
     ).astype(jnp.bfloat16)
-    w_full = lax.all_gather(w_o, "col", axis=1, tiled=True)
+    w_full = fix_area(w_o, "col")
     key_heads = keys_vals[:, :width_d].reshape(-1, HEADS, HEAD)
     val_heads = keys_vals[:, width_d:].reshape(-1, HEADS, HEAD)
     query_heads = queries.reshape(latent_count, HEADS, HEAD)

time: 480 us -> 465 us (0.969)
  waiting for transfers between devices: 334 us -> 308 us
  starting transfers between devices: 8.75 us -> 16.8 us
    all_gather x1 -> x0, waiting for transfers between devices: 30.1 us -> none  [body(): w_full = lax.all_gather(w_o, 'col', axis=1, tiled=True)]
    ppermute x0 -> x3, waiting for transfers between devices: none -> 24.6 us  [fix_area(): series.append(lax.ppermute(series[-1], comm_axis, frames))]
    reduce_scatter x1, waiting for transfers between devices: 34.6 us -> 16 us  [body(): lax.psum_scatter(num_terms, 'col', scatter_dimension=0, tiled=True)]
    ppermute x0 -> x3, starting transfers between devices: none -> 8.11 us  [fix_area(): series.append(lax.ppermute(series[-1], comm_axis, frames))]
  transfers between devices with their start and end apart: 11 -> 13, of which waited for: 10 -> 11; matrix products, arithmetic and copies ran while one was open for 5% -> 5% of each run, Pallas kernels for 0% -> 0%
where the time goes in v1:
time: 465 us
  waiting for transfers between devices  308 us (66%)
  blocking collectives  70.7 us (15%)
  matrix products  24.2 us (5%)
  other arithmetic  21.3 us (5%)
  starting transfers between devices  16.8 us (4%)
  between operations  14.5 us (3%)
  local copies, waits for them, and re-layouts  8.66 us (2%)
    all_gather x1, waiting for transfers between devices, body(): lax.all_gather(w_out, 'col', axis=0, tiled=True)  89.4 us
    all_gather x1, waiting for transfers between devices, body(): lax.all_gather(w_in, 'col', axis=1, tiled=True)  57.7 us
    psum x1, waiting for transfers between devices, body(): den_share, num_share = lax.psum((den_part, num_part), 'row')  43.3 us
    all_gather x1, waiting for transfers between devices, body(): lax.all_gather(w_kv, 'col', axis=1, tiled=True)  42.4 us
    pmax x1, blocking collectives, body(): peak = lax.pmax(maxima, ('row', 'col'))  39 us
    ppermute x3, waiting for transfers between devices, fix_area(): series.append(lax.ppermute(series[-1], comm_axis, frames))  24.6 us
    reduce_scatter x1, waiting for transfers between devices, body(): lax.psum_scatter(den_terms, 'col', scatter_dimension=0, tiled=True)  19.6 us
    all_gather x1, blocking collectives, body(): latents = lax.all_gather(own_rows, 'col', axis=0, tiled=True)  19.5 us
  transfers between devices with their start and end apart: 13, of which 11 were waited for; matrix products, arithmetic and copies ran while one was open for 5% of the time, Pallas kernels for 0%

profile of v1, /device:TPU:0, one launch (start us, length us, event | category | flops | bytes accessed | tf_op | source)
XLA Modules:
  0.0 464.7 jit_solution(7584691104339381945)
XLA Ops:
  8.8 2.4 collective-permute-start
  11.2 1.3 collective-permute-start.1
  14.1 2.3 collective-permute-done.1
  16.6 3.5 collective-permute-start.2
  21.5 4.3 collective-permute-done.2
  25.8 7.4 %collective-permute-done.3 = bf16[22,3,768]{2,1,0:T(4,128)(2,1)S(1)} collective-permute-done((bf16[22,3,768]{2,1,0:T(4,128)(2,1)S(1)}, bf16[22,3,768]{2,1,0:T(4,128)(2,1)S(1)}, u32[]{:S(2)}, u32[]{:S(2)}) %collective-permute-start.3) | collective-permute-done | bytes 101408 | tf_op jit(solution)/shard_map/ppermute | solution.py:27
  33.6 12.3 %fusion.111 = (f32[16,24]{1,0:T(8,128)S(1)}, f32[16,24,768]{2,1,0:T(8,128)S(1)}) fusion(f32[768]{0:T(1024)S(1)} %get-tuple-element.49, f32[22,30,768]{2,1,0:T(8,128)S(1)} %maximum_convert_fusion, f32[768]{0:T(1024)S(1)} %get-tuple-element.50, f32[768]{0:T(1024)S(1)} %get-tuple-element.3, f32[768]{0:T(1024)S(1)} %get-tuple-element.4, ...), kind=kLoop, calls=%fused_computation.227 | loop fusion | flops 28900992 | bytes 59134464 | tf_op jit(solution)/shard_map/reduce_sum | solution.py:47
  46.8 57.7 %all-gather.4.cloned.1.call-done = bf16[768,3072]{1,0:T(8,128)(2,1)} async-done(((bf16[768,768]{1,0:T(8,128)(2,1)}), bf16[768,3072]{1,0:T(8,128)(2,1)}) %all-gather.4.cloned.1.call-update) | async-done | bytes 4718608 | tf_op jit(solution)/shard_map/all_gather | solution.py:80
  104.6 89.4 %all-gather.6.cloned.1.call-done = bf16[3072,768]{1,0:T(8,128)(2,1)} async-done(((bf16[768,768]{1,0:T(8,128)(2,1)}), bf16[3072,768]{1,0:T(8,128)(2,1)}) %all-gather.6.cloned.1.call-update) | async-done | bytes 4718608 | tf_op jit(solution)/shard_map/all_gather | solution.py:85
  193.9 7.9 %fusion.34 = bf16[384,768]{1,0:T(8,128)(2,1)S(1)} fusion(bf16[3072,768]{1,0:T(8,128)(2,1)} %all-gather.6.cloned.1.call-done, bf16[384,768]{1,0:T(8,128)(2,1)S(1)} %bitcast.76, bf16[384,768]{1,0:T(8,128)(2,1)S(1)} %bitcast.80, bf16[768,3072]{1,0:T(8,128)(2,1)} %all-gather.4.cloned.1.call-done), kind=kOutput, calls=%fused_computation.38 | convolution fusion | flops 3635380224 | bytes 11206656 | tf_op jit(solution)/shard_map/dot_general | solution.py:84
  201.9 42.4 %all-gather.8.cloned.1.call-done = bf16[768,1536]{1,0:T(8,128)(2,1)} async-done(((bf16[768,384]{1,0:T(8,128)(2,1)}), bf16[768,1536]{1,0:T(8,128)(2,1)}) %all-gather.8.cloned.1.call-update) | async-done | bytes 2359312 | tf_op jit(solution)/shard_map/all_gather | solution.py:91
  244.2 2.7 convolution_convert_fusion
  248.9 1.8 bitcast_reduce_fusion
  250.8 2.3 bitcast_reduce_fusion.1
  253.0 2.3 bitcast_reduce_fusion.2
  255.4 2.1 copy.22
  257.5 3.6 fusion.37
  261.1 3.0 fusion.11
  264.1 1.5 fusion.40
  266.2 1.5 fusion.43
  267.6 39.0 %pmax.7 = f32[512,12]{0,1:T(8,128)S(1)} all-reduce(f32[512,12]{0,1:T(8,128)S(1)} %pad_maximum_fusion.1), channel_id=1, replica_groups=mesh['row'=8,'col'=4] {'row','col'}, use_global_device_ids=true, to_apply=%region_5.6 | all-reduce | flops 6144 | bytes 49152 | tf_op jit(solution)/shard_map/pmax | solution.py:126
  307.3 2.7 maximum_multiply_fusion
  310.9 1.7 collective-permute-start.4
  312.6 10.9 %collective-permute-done.4 = bf16[768,192]{0,1:T(8,128)(2,1)S(1)} collective-permute-done((bf16[768,192]{0,1:T(8,128)(2,1)S(1)}, bf16[768,192]{0,1:T(8,128)(2,1)S(1)}, u32[]{:S(2)}, u32[]{:S(2)}) %collective-permute-start.4) | collective-permute-done | bytes 294944 | tf_op jit(solution)/shard_map/ppermute | solution.py:66
  323.5 2.5 collective-permute-start.5
  325.9 13.8 %collective-permute-done.5 = bf16[768,192]{0,1:T(8,128)(2,1)S(1)} collective-permute-done((bf16[768,192]{0,1:T(8,128)(2,1)S(1)}, bf16[768,192]{0,1:T(8,128)(2,1)S(1)}, u32[]{:S(2)}, u32[]{:S(2)}) %collective-permute-start.5) | collective-permute-done | bytes 294944 | tf_op jit(solution)/shard_map/ppermute | solution.py:66
  339.7 4.0 collective-permute-start.6
  343.8 16.0 %reduce-scatter.3.cloned.1.call-done = f32[128,768]{0,1:T(8,128)} async-done(((f32[512,768]{0,1:T(8,128)}), f32[128,768]{0,1:T(8,128)}) %reduce-scatter.3.cloned.1.call-update) | async-done | bytes 393232 | tf_op jit(solution)/shard_map/reduce_scatter | solution.py:132
  360.6 19.6 %reduce-scatter.5.cloned.1.call-done = f32[128,12]{0,1:T(8,128)} async-done(((f32[512,12]{0,1:T(8,128)}), f32[128,12]{0,1:T(8,128)}) %reduce-scatter.5.cloned.1.call-update) | async-done | bytes 6160 | tf_op jit(solution)/shard_map/reduce_scatter | solution.py:131
  380.2 12.2 %psum.15 = f32[128,12]{0,1:T(8,128)S(1)} all-reduce(f32[128,12]{0,1:T(8,128)} %reduce-scatter.5.cloned.1.call-done), channel_id=1, replica_groups=mesh['row'=8,'col'=4] {'row'}, use_global_device_ids=true, to_apply=%region_12.13 | all-reduce | flops 1536 | bytes 12288 | tf_op jit(solution)/shard_map/psum | solution.py:134
  392.4 43.3 %all-reduce.2.cloned.1.call-done = f32[128,768]{0,1:T(8,128)} async-done(((f32[128,768]{0,1:T(8,128)}), f32[128,768]{0,1:T(8,128)}) %all-reduce.2.cloned.1.call-update) | async-done | bytes 393232 | tf_op jit(solution)/shard_map/psum | solution.py:134
  437.5 19.5 %all_gather.15 = bf16[512,768]{1,0:T(8,128)(2,1)S(1)} all-gather(bf16[128,768]{1,0:T(8,128)(2,1)S(1)} %convolution_convert_fusion.1), channel_id=1, replica_groups=mesh['row'=8,'col'=4] {'col'}, dimensions={0}, use_global_device_ids=true | all-gather | bytes 983040 | tf_op jit(solution)/shard_map/all_gather | solution.py:138
  (66 shorter events, 13.5 us)
Async XLA Ops:
  7.2 1.6 copy-start.1
  7.2 97.4 %all-gather.4.cloned.1.call-start = ((), (), s32[]{:S(2)}) async-start(), calls=%async_computation.2 | async-start | bytes 5898240 | tf_op jit(solution)/shard_map/all_gather | solution.py:80
  7.9 4.6 copy-start.7
  7.9 4.8 %copy-start.2 = (bf16[512,768]{1,0:T(8,128)(2,1)S(1)}, bf16[512,768]{1,0:T(8,128)(2,1)}, u32[]{:S(2)}) copy-start(bf16[512,768]{1,0:T(8,128)(2,1)} %param.17) | copy-start | bytes 2359300
  7.9 186.0 %all-gather.6.cloned.1.call-start = ((), (), s32[]{:S(2)}) async-start(), calls=%async_computation.3 | async-start | bytes 5898240 | tf_op jit(solution)/shard_map/all_gather | solution.py:85
  8.7 235.6 %all-gather.8.cloned.1.call-start = ((), (), s32[]{:S(2)}) async-start(), calls=%async_computation.4 | async-start | bytes 2949120 | tf_op jit(solution)/shard_map/all_gather | solution.py:91
  8.8 5.3 %collective-permute-start = (bf16[3,24,768]{2,1,0:T(8,128)(2,1)S(1)}, bf16[3,24,768]{2,1,0:T(8,128)(2,1)S(1)}, u32[]{:S(2)}, u32[]{:S(2)}) collective-permute-start(bf16[3,24,768]{2,1,0:T(8,128)(2,1)S(1)} %get-tuple-element.62), channel_id=1, source_target_pairs={{0,4},{4,8},{8,12},{12,16},{16,20},{20,24},{24,28},{1,5},{5,9},{9,... | collective-permute-start | bytes 331784 | tf_op jit(solution)/shard_map/ppermute | solution.py:25
  11.2 5.3 %collective-permute-start.1 = (bf16[3,24,768]{2,1,0:T(8,128)(2,1)S(1)}, bf16[3,24,768]{2,1,0:T(8,128)(2,1)S(1)}, u32[]{:S(2)}, u32[]{:S(2)}) collective-permute-start(bf16[3,24,768]{2,1,0:T(8,128)(2,1)S(1)} %get-tuple-element.61), channel_id=1, source_target_pairs={{4,0},{8,4},{12,8},{16,12},{20,16},{24,20},{28,24},{5,1},{9,5},{13... | collective-permute-start | bytes 331784 | tf_op jit(solution)/shard_map/ppermute | solution.py:27
  12.5 347.2 %reduce-scatter.3.cloned.1.call-start = ((), (), s32[]{:S(2)}) async-start(), calls=%async_computation.5 | async-start | bytes 1966080 | tf_op jit(solution)/shard_map/reduce_scatter | solution.py:132
  16.6 9.2 %collective-permute-start.2 = (bf16[22,3,768]{2,1,0:T(4,128)(2,1)S(1)}, bf16[22,3,768]{2,1,0:T(4,128)(2,1)S(1)}, u32[]{:S(2)}, u32[]{:S(2)}) collective-permute-start(bf16[22,3,768]{2,1,0:T(4,128)(2,1)S(1)} %get-tuple-element.59), channel_id=1, source_target_pairs={{0,1},{1,2},{2,3},{4,5},{5,6},{6,7},{8,9},{9,10},{10,11},{12,13},{... | collective-permute-start | bytes 304136 | tf_op jit(solution)/shard_map/ppermute | solution.py:25
  20.1 13.1 %collective-permute-start.3 = (bf16[22,3,768]{2,1,0:T(4,128)(2,1)S(1)}, bf16[22,3,768]{2,1,0:T(4,128)(2,1)S(1)}, u32[]{:S(2)}, u32[]{:S(2)}) collective-permute-start(bf16[22,3,768]{2,1,0:T(4,128)(2,1)S(1)} %get-tuple-element.60), channel_id=1, source_target_pairs={{1,0},{2,1},{3,2},{5,4},{6,5},{7,6},{9,8},{10,9},{11,10},{13,12},{... | collective-permute-start | bytes 304136 | tf_op jit(solution)/shard_map/ppermute | solution.py:27
  45.9 0.7 copy-start.8
  45.9 0.7 copy-start.9
  201.9 45.1 %copy-start.11 = (bf16[384,768]{1,0:T(8,128)(2,1)}, bf16[384,768]{1,0:T(8,128)(2,1)S(1)}, u32[]{:S(2)}) copy-start(bf16[384,768]{1,0:T(8,128)(2,1)S(1)} %fusion.34) | copy-start | bytes 1769476
  248.9 1.8 copy-start.3
  248.9 1.8 copy-start.5
  257.5 3.6 copy-start
  261.1 3.0 copy-start.4
  310.0 1.0 copy-start.6
  310.0 70.2 %reduce-scatter.5.cloned.1.call-start = ((), (), s32[]{:S(2)}) async-start(), calls=%async_computation.7 | async-start | bytes 40960 | tf_op jit(solution)/shard_map/reduce_scatter | solution.py:131
  310.9 12.5 %collective-permute-start.4 = (bf16[768,192]{0,1:T(8,128)(2,1)S(1)}, bf16[768,192]{0,1:T(8,128)(2,1)S(1)}, u32[]{:S(2)}, u32[]{:S(2)}) collective-permute-start(bf16[768,192]{0,1:T(8,128)(2,1)S(1)} %copy-done.6), channel_id=1, source_target_pairs={{0,1},{1,2},{2,3},{3,0},{4,5},{5,6},{6,7},{7,4},{8,9},{9,10},{10,1... | collective-permute-start | bytes 884744 | tf_op jit(solution)/shard_map/ppermute | solution.py:66
  323.5 16.2 %collective-permute-start.5 = (bf16[768,192]{0,1:T(8,128)(2,1)S(1)}, bf16[768,192]{0,1:T(8,128)(2,1)S(1)}, u32[]{:S(2)}, u32[]{:S(2)}) collective-permute-start(bf16[768,192]{0,1:T(8,128)(2,1)S(1)} %collective-permute-done.4), channel_id=1, source_target_pairs={{0,1},{1,2},{2,3},{3,0},{4,5},{5,6},{6,7},{7,4},{8,9},{9,10},{10,1... | collective-permute-start | bytes 884744 | tf_op jit(solution)/shard_map/ppermute | solution.py:66
  339.7 20.0 %collective-permute-start.6 = (bf16[768,192]{0,1:T(8,128)(2,1)S(1)}, bf16[768,192]{0,1:T(8,128)(2,1)S(1)}, u32[]{:S(2)}, u32[]{:S(2)}) collective-permute-start(bf16[768,192]{0,1:T(8,128)(2,1)S(1)} %collective-permute-done.5), channel_id=1, source_target_pairs={{0,1},{1,2},{2,3},{3,0},{4,5},{5,6},{6,7},{7,4},{8,9},{9,10},{10,1... | collective-permute-start | bytes 884744 | tf_op jit(solution)/shard_map/ppermute | solution.py:66
  343.7 92.0 %all-reduce.2.cloned.1.call-start = ((), (), s32[]{:S(2)}) async-start(), calls=%async_computation.6 | async-start | bytes 786432 | tf_op jit(solution)/shard_map/psum | solution.py:134
  359.9 76.9 %copy-start.10 = (f32[768]{0:T(1024)S(1)}, f32[768]{0:T(1024)}, u32[]{:S(2)}) copy-start(f32[768]{0:T(1024)} %param.18) | copy-start | bytes 9220
Sparse Core Ops, SparseCore 0:
  9.6 94.9 all-gather.3
  106.1 87.7 all-gather.5
  195.6 48.6 all-gather.7
  310.1 49.5 reduce-scatter.2
  361.8 18.3 reduce-scatter.4
  383.1 52.5 all-reduce.1
